TPU v7x, 32 devices: a whole 2x2x4 slice. The times are simulated.
32 devices in a mesh: req: 4 (over z), tok: 8 (over y, x, core).
Axes of the slice: x: 2, y: 2, z: 4, core: 2. Of those that a mesh axis runs over, the one named last changes fastest.
Arguments:
- hidden_in: bfloat16 [4096, 2048], P(('req', 'tok')), may hold values from -1.5 to 1.5
- suffix_len: int32 [4, 4], P('req'), may hold values from 1 to 512, 1024 in all within a row
- prefix_of: int32 [4, 4], P('req'), may hold values from 0 to 3
- prefix_slot: int32 [4], replicated, may hold values from 0 to 3, each once
- prefix_cache: bfloat16 [4, 4, 2048, 128], P('req', None, 'tok'), may hold values from -160 to 160
- attn_gain: bfloat16 [2048], replicated, may hold values from 0.099609375 to 1.8984375
- query_weight: bfloat16 [2048, 2048], P(None, 'tok'), may hold values from -0.125 to 0.125
- keyval_weight: bfloat16 [4, 2048, 128], replicated, may hold values from -0.125 to 0.125
- out_weight: bfloat16 [2048, 2048], P('tok'), may hold values from -0.125 to 0.125
- mlp_gain: bfloat16 [2048], replicated, may hold values from 0.099609375 to 1.8984375
- gate_weight: bfloat16 [2048, 4096], P(None, 'req'), may hold values from -0.125 to 0.125
- up_weight: bfloat16 [2048, 4096], P(None, 'req'), may hold values from -0.125 to 0.125
- down_weight: bfloat16 [4096, 2048], P('req'), may hold values from -0.09375 to 0.09375
- final_gain: bfloat16 [2048], replicated, may hold values from 0.099609375 to 1.8984375
- head_weight: bfloat16 [32000, 2048], P('tok'), may hold values from -7 to 7
Outputs:
- hidden_out: bfloat16 [4096, 2048], P(('req', 'tok'))
- suffix_cache: bfloat16 [4096, 512], P('req', 'tok')
- last_rms: float32 [4, 4], P('req')
- top_logit: float32 [4, 4], P('req')
- log_total: float32 [4, 4], P('req')
Inputs may be any that keep to these rules, and one draw needn't show every extreme that they name: `suffix_len`: each owner's 4 lengths sum to 1024, and the largest of each owner is 512.
All inputs are finite; a program needn't handle non-finite values.
Results may differ from a plain program's by a relative error of at most 0.02.
Values may be sent and summed in bfloat16 or wider, within the bound.
A program may use at most 128 MiB of HBM per device.

v0:
```python
import math
import jax
import jax.numpy as jnp
from jax import lax
from jax.sharding import PartitionSpec as P

HD = 64
PRE_LEN = 16384
epsilon = 1e-05
neg_large = -1e30


def rms_scale(values, gain_vec):
    widened = values.astype(jnp.float32)
    mean_square = jnp.mean(widened * widened, axis=-1, keepdims=True)
    return widened * lax.rsqrt(mean_square + epsilon) * gain_vec.astype(jnp.float32)


def rotate(vectors, positions):
    half_width = vectors.shape[-1] // 2
    levels = jnp.arange(half_width).astype(jnp.float32)
    inverse = jnp.exp(levels * (-2.0 * math.log(10000.0) / vectors.shape[-1]))
    angles = positions.astype(jnp.float32)[:, None] * inverse[None, :]
    cosine = jnp.cos(angles)[:, None, :]
    sine_part = jnp.sin(angles)[:, None, :]
    first_half = vectors[..., :half_width]
    second_half = vectors[..., half_width:]
    return jnp.concatenate(
        [
            first_half * cosine - second_half * sine_part,
            second_half * cosine + first_half * sine_part,
        ],
        axis=-1,
    )


def owner_layout(lengths, row_count):
    end_rows = jnp.cumsum(lengths)
    starts = end_rows - lengths
    row_index = jnp.arange(row_count)
    member = (row_index[:, None] >= starts[None, :]) & (row_index[:, None] < end_rows[None, :])
    offsets = row_index - jnp.sum(jnp.where(member, starts[None, :], 0), axis=1)
    return (starts, end_rows, offsets)


def slot_lookup(chosen, prefix_slot):
    table_index = jnp.arange(prefix_slot.shape[0])
    hits = chosen[:, None] == table_index[None, :]
    return jnp.sum(jnp.where(hits, prefix_slot[None, :], 0), axis=1)


def request_attention(query_block, suffix_block, window, live_len):
    row_count = query_block.shape[0]
    head_width = query_block.shape[-1]
    window_len = window.shape[1]
    suffix_major = jnp.transpose(suffix_block, (1, 0, 2))
    key_rows = jnp.concatenate([window[:, :, :head_width], suffix_major[:, :, :head_width]], axis=1)
    value_rows = jnp.concatenate(
        [window[:, :, head_width:], suffix_major[:, :, head_width:]], axis=1
    )
    scores = jnp.einsum(
        "rgke,gse->gkrs", query_block, key_rows, preferred_element_type=jnp.float32
    ) * head_width ** (-0.5)
    row_index = jnp.arange(row_count)
    prefix_seen = jnp.arange(window_len)[None, :] > row_index[:, None]
    suffix_seen = (
        (row_index[None, :] <= row_index[:, None])
        & (row_index[:, None] - row_index[None, :] < window_len)
        & (row_index[None, :] < live_len)
    )
    visible = jnp.concatenate([prefix_seen, suffix_seen], axis=1)
    masked = jnp.where(visible, scores, neg_large)
    highest = jnp.max(masked, axis=-1, keepdims=True)
    weights = jnp.where(visible, jnp.exp(masked - highest), 0.0)
    totals = jnp.sum(weights, axis=-1, keepdims=True)
    totals = jnp.where(row_index[:, None] < live_len, totals, 1.0)
    rounded = weights.astype(jnp.bfloat16)
    mixed_rows = jnp.einsum(
        "gkrs,gse->rgke", rounded, value_rows, preferred_element_type=jnp.float32
    )
    mixed_rows = mixed_rows / jnp.transpose(totals, (2, 0, 1, 3))
    return mixed_rows.reshape(row_count, -1).astype(jnp.bfloat16)


def shards(
    hidden_in,
    suffix_len,
    prefix_of,
    prefix_slot,
    prefix_cache,
    attn_gain,
    query_weight,
    keyval_weight,
    out_weight,
    mlp_gain,
    gate_weight,
    up_weight,
    down_weight,
    final_gain,
    head_weight,
):
    tok_count = lax.axis_size("tok")
    tok_place = lax.axis_index("tok")
    tok_rows = hidden_in.shape[0]
    own_rows = tok_rows * tok_count
    most_rows = own_rows // 2
    heads_here = query_weight.shape[1] // HD
    kv_count = keyval_weight.shape[0]
    kv_head = tok_place * kv_count // tok_count
    repeat_count = tok_count // kv_count
    lengths = suffix_len[0]
    starts, end_rows, offsets = owner_layout(lengths, own_rows)
    positions = offsets + PRE_LEN
    normed = rms_scale(hidden_in, attn_gain).astype(jnp.bfloat16)
    kv_weight = lax.dynamic_index_in_dim(keyval_weight, kv_head, 0, keepdims=False)
    united_weight = jnp.concatenate([query_weight, kv_weight], axis=1)
    projected = jnp.dot(
        lax.all_gather(normed, "tok", axis=0, tiled=True),
        united_weight,
        preferred_element_type=jnp.float32,
    )
    queries = rotate(
        projected[:, : heads_here * HD].reshape(own_rows, heads_here, HD), positions
    ).astype(jnp.bfloat16)
    keyvals = projected[:, heads_here * HD :].reshape(own_rows, 1, 2 * HD)
    rotated = rotate(keyvals[:, :, :HD], positions)
    keyvals = jnp.concatenate([rotated, keyvals[:, :, HD:]], axis=-1).astype(jnp.bfloat16)
    cache_width = kv_count * 2 * HD // tok_count
    cache_offset = tok_place * cache_width % (2 * HD)
    suffix_cache = lax.dynamic_slice_in_dim(keyvals[:, 0, :], cache_offset, cache_width, 1)
    every_owner = lax.all_gather(prefix_cache, "req", axis=0, tiled=True)
    routed = jnp.repeat(every_owner, repeat_count, axis=1)
    windows = lax.all_to_all(routed, "tok", split_axis=1, concat_axis=2, tiled=True)
    windows = windows[:, 0]
    padded_queries = jnp.concatenate(
        [queries, jnp.zeros((most_rows, heads_here, HD), jnp.bfloat16)], axis=0
    )
    padded_keyvals = jnp.concatenate(
        [keyvals, jnp.zeros((most_rows, 1, 2 * HD), jnp.bfloat16)], axis=0
    )
    cache_rows = slot_lookup(prefix_of[0], prefix_slot)

    def one_request(buffer, request):
        first_row, live_len, cache_row = request
        query_block = lax.dynamic_slice_in_dim(padded_queries, first_row, most_rows, 0).reshape(
            most_rows, 1, heads_here, HD
        )
        suffix_block = lax.dynamic_slice_in_dim(padded_keyvals, first_row, most_rows, 0)
        window = lax.dynamic_index_in_dim(windows, cache_row, 0, keepdims=True)
        mixed_rows = request_attention(query_block, suffix_block, window, live_len)
        current = lax.dynamic_slice_in_dim(buffer, first_row, most_rows, 0)
        keep_rows = jnp.arange(most_rows)[:, None] < live_len
        return (
            lax.dynamic_update_slice_in_dim(
                buffer, jnp.where(keep_rows, mixed_rows, current), first_row, 0
            ),
            None,
        )

    buffer = jnp.zeros((own_rows + most_rows, heads_here * HD), jnp.bfloat16)
    buffer, unused = lax.scan(one_request, buffer, (starts, lengths, cache_rows))
    attended = buffer[:own_rows]
    projected_back = lax.psum_scatter(
        jnp.dot(attended, out_weight, preferred_element_type=jnp.float32).astype(jnp.bfloat16),
        "tok",
        scatter_dimension=0,
        tiled=True,
    ).astype(jnp.float32)
    middle = (hidden_in.astype(jnp.float32) + projected_back).astype(jnp.bfloat16)
    mlp_in = rms_scale(middle, mlp_gain).astype(jnp.bfloat16)
    shard_part = lax.all_gather(mlp_in, "req", axis=0, tiled=True)
    gate_proj = jnp.dot(shard_part, gate_weight, preferred_element_type=jnp.float32)
    lifted = jnp.dot(shard_part, up_weight, preferred_element_type=jnp.float32)
    hidden_act = (jax.nn.silu(gate_proj) * lifted).astype(jnp.bfloat16)
    summed = lax.psum_scatter(
        jnp.dot(hidden_act, down_weight, preferred_element_type=jnp.float32).astype(jnp.bfloat16),
        "req",
        scatter_dimension=0,
        tiled=True,
    ).astype(jnp.float32)
    final_state = (middle.astype(jnp.float32) + summed).astype(jnp.bfloat16)
    local_index = jnp.arange(tok_rows) + tok_place * tok_rows
    picker = (local_index[None, :] == (end_rows - 1)[:, None]).astype(jnp.bfloat16)
    picked = jnp.dot(picker, final_state, preferred_element_type=jnp.float32)
    last_rows = lax.psum(picked.astype(jnp.bfloat16), "tok").astype(jnp.float32)
    mean_square = jnp.mean(last_rows * last_rows, axis=-1, keepdims=True)
    spread = jnp.sqrt(mean_square + epsilon)
    final_normed = (
        last_rows * lax.rsqrt(mean_square + epsilon) * final_gain.astype(jnp.float32)
    ).astype(jnp.bfloat16)
    logits = lax.dot_general(
        final_normed, head_weight, (((1,), (1,)), ((), ())), preferred_element_type=jnp.float32
    )
    highest = lax.pmax(jnp.max(logits, axis=-1), "tok")
    summed_exp = lax.psum(jnp.sum(jnp.exp(logits - highest[:, None]), axis=-1), "tok")
    log_total = highest + jnp.log(summed_exp)
    return (final_state, suffix_cache, spread[:, 0][None, :], highest[None, :], log_total[None, :])


def solution(mesh):
    placed = (
        P(("req", "tok"), None),
        P("req", None),
        P("req", None),
        P(),
        P("req", None, "tok", None),
        P(),
        P(None, "tok"),
        P(),
        P("tok", None),
        P(),
        P(None, "req"),
        P(None, "req"),
        P("req", None),
        P(),
        P("tok", None),
    )
    return jax.shard_map(
        shards,
        mesh=mesh,
        in_specs=placed,
        out_specs=(
            P(("req", "tok"), None),
            P("req", "tok"),
            P("req", None),
            P("req", None),
            P("req", None),
        ),
        check_vma=False,
    )
```

profile of v0, /device:TPU:0, one launch (start us, length us, event | category | flops | bytes accessed | tf_op | source)
XLA Modules:
  0.0 462.7 jit_solution(11795564161702369459)
XLA Ops:
  11.9 28.3 %all-gather.4.cloned.1.call-done = bf16[4,4,256,128]{3,2,1,0:T(8,128)(2,1)} async-done(((bf16[1,4,256,128]{3,2,1,0:T(8,128)(2,1)}), bf16[4,4,256,128]{3,2,1,0:T(8,128)(2,1)}) %all-gather.4.cloned.1.call-update) | async-done | bytes 1048592 | tf_op jit(solution)/shard_map/all_gather | solution.py:131
  51.9 29.2 %all-to-all-done = bf16[4,8,256,128]{2,3,0,1:T(8,128)(2,1)} async-done(((bf16[4,8,256,128]{2,3,0,1:T(8,128)(2,1)}), bf16[4,8,256,128]{2,3,0,1:T(8,128)(2,1)}, u32[]{:S(2)}, u32[]{:S(2)}) %all-to-all-start) | async-done | bytes 2097184 | tf_op jit(solution)/shard_map/all_to_all | solution.py:133
  84.2 8.7 %all-gather.6.cloned.1.call-done = bf16[1024,2048]{1,0:T(8,128)(2,1)} async-done(((bf16[128,2048]{1,0:T(8,128)(2,1)}), bf16[1024,2048]{1,0:T(8,128)(2,1)}) %all-gather.6.cloned.1.call-update) | async-done | bytes 4194320 | tf_op jit(solution)/shard_map/all_gather | solution.py:118
  101.5 129.9 %while.10 = (s32[]{:T(128)}, bf16[1536,256]{0,1:T(8,128)(2,1)}, s32[4]{0:T(128)}, s32[4]{0:T(128)}, bf16[4,2048,128]{2,1,0:T(8,128)(2,1)S(1)}, /*index=5*/s32[4]...) while((s32[]{:T(128)}, bf16[1536,256]{0,1:T(8,128)(2,1)}, ...), condition=%wide.region_7.8_spmd, body=%wide.region_4.7_spmd.sunk | while | flops 1415707136 | bytes 83556792 | solution.py:161
  113.6 4.7 %fusion.93 = (f32[4,512]{1,0:T(4,128)S(1)}, f32[2560,512,4]{1,0,2:T(8,128)S(1)}) fusion(pred[512,2560]{0,1:T(8,128)(4,1)S(1)} %pad_add_fusion.2, bf16[1536,4,64]{0,2,1:T(8,128)(2,1)} %get-tuple-element.192, s32[]{:T(128)S(6)} %select_n.119, bf16[1,512,64]{1,2,0:T(8,128)(2,1)S(1)} %copy-done.10, bf16[1,2048,64]{1,2,0:T(8,128)(2,1)S(1)} %copy-done.5), kind=kOutput, calls=%fused_computation.2.clone.1 | convolution fusion | flops 687470592 | bytes 22880260 | tf_op jit(solution)/shard_map/while/body/eval_jaxpr/rgke,gse->gkrs/dot_general | solution.py:61
  118.3 5.2 %fusion.94 = f32[4,512]{1,0:T(4,128)S(1)} fusion(f32[2560,512,4]{1,0,2:T(8,128)S(1)} %get-tuple-element.155, f32[4,512]{1,0:T(4,128)S(1)} %get-tuple-element.156, pred[512,2560]{0,1:T(8,128)(4,1)S(1)} %pad_add_fusion.2), kind=kLoop, calls=%fused_computation.3.clone.1 | loop fusion | flops 26212352 | bytes 22298624 | tf_op jit(solution)/shard_map/while/body/eval_jaxpr/reduce_sum | solution.py:75
  123.6 5.9 %fusion.96 = bf16[512,1,4,64]{0,3,2,1:T(8,128)(2,1)S(1)} fusion(f32[2560,512,4]{1,0,2:T(8,128)S(1)} %get-tuple-element.155, f32[4,512]{1,0:T(4,128)S(1)} %get-tuple-element.156, pred[512,2560]{0,1:T(8,128)(4,1)S(1)} %pad_add_fusion.2, bf16[1,512,64]{1,2,0:T(8,128)(2,1)S(1)} %get-tuple-element.157, bf16[1,2048,64]{1,2,0:T(8,128)(2,1)S(1)} %copy.39, ...), kind=kOutput, calls=%fused_computation.17.clone.1 | convolution fusion | flops 698220544 | bytes 22888448 | tf_op jit(solution)/shard_map/while/body/eval_jaxpr/gkrs,gse->rgke/dot_general | solution.py:78
  150.5 5.2 %fusion.94 = f32[4,512]{1,0:T(4,128)S(1)} fusion(f32[2560,512,4]{1,0,2:T(8,128)S(1)} %get-tuple-element.155, f32[4,512]{1,0:T(4,128)S(1)} %get-tuple-element.156, pred[512,2560]{0,1:T(8,128)(4,1)S(1)} %pad_add_fusion.2), kind=kLoop, calls=%fused_computation.3.clone.1 | loop fusion | flops 26212352 | bytes 22298624 | tf_op jit(solution)/shard_map/while/body/eval_jaxpr/reduce_sum | solution.py:75
  155.7 5.9 %fusion.96 = bf16[512,1,4,64]{0,3,2,1:T(8,128)(2,1)S(1)} fusion(f32[2560,512,4]{1,0,2:T(8,128)S(1)} %get-tuple-element.155, f32[4,512]{1,0:T(4,128)S(1)} %get-tuple-element.156, pred[512,2560]{0,1:T(8,128)(4,1)S(1)} %pad_add_fusion.2, bf16[1,512,64]{1,2,0:T(8,128)(2,1)S(1)} %get-tuple-element.157, bf16[1,2048,64]{1,2,0:T(8,128)(2,1)S(1)} %copy.39, ...), kind=kOutput, calls=%fused_computation.17.clone.1 | convolution fusion | flops 698220544 | bytes 22888448 | tf_op jit(solution)/shard_map/while/body/eval_jaxpr/gkrs,gse->rgke/dot_general | solution.py:78
  178.6 4.7 %fusion.93 = (f32[4,512]{1,0:T(4,128)S(1)}, f32[2560,512,4]{1,0,2:T(8,128)S(1)}) fusion(pred[512,2560]{0,1:T(8,128)(4,1)S(1)} %pad_add_fusion.2, bf16[1536,4,64]{0,2,1:T(8,128)(2,1)} %get-tuple-element.192, s32[]{:T(128)S(6)} %select_n.119, bf16[1,512,64]{1,2,0:T(8,128)(2,1)S(1)} %copy-done.10, bf16[1,2048,64]{1,2,0:T(8,128)(2,1)S(1)} %copy-done.5), kind=kOutput, calls=%fused_computation.2.clone.1 | convolution fusion | flops 687470592 | bytes 22880260 | tf_op jit(solution)/shard_map/while/body/eval_jaxpr/rgke,gse->gkrs/dot_general | solution.py:61
  183.3 5.2 %fusion.94 = f32[4,512]{1,0:T(4,128)S(1)} fusion(f32[2560,512,4]{1,0,2:T(8,128)S(1)} %get-tuple-element.155, f32[4,512]{1,0:T(4,128)S(1)} %get-tuple-element.156, pred[512,2560]{0,1:T(8,128)(4,1)S(1)} %pad_add_fusion.2), kind=kLoop, calls=%fused_computation.3.clone.1 | loop fusion | flops 26212352 | bytes 22298624 | tf_op jit(solution)/shard_map/while/body/eval_jaxpr/reduce_sum | solution.py:75
  188.5 5.9 %fusion.96 = bf16[512,1,4,64]{0,3,2,1:T(8,128)(2,1)S(1)} fusion(f32[2560,512,4]{1,0,2:T(8,128)S(1)} %get-tuple-element.155, f32[4,512]{1,0:T(4,128)S(1)} %get-tuple-element.156, pred[512,2560]{0,1:T(8,128)(4,1)S(1)} %pad_add_fusion.2, bf16[1,512,64]{1,2,0:T(8,128)(2,1)S(1)} %get-tuple-element.157, bf16[1,2048,64]{1,2,0:T(8,128)(2,1)S(1)} %copy.39, ...), kind=kOutput, calls=%fused_computation.17.clone.1 | convolution fusion | flops 698220544 | bytes 22888448 | tf_op jit(solution)/shard_map/while/body/eval_jaxpr/gkrs,gse->rgke/dot_general | solution.py:78
  211.4 4.7 %fusion.93 = (f32[4,512]{1,0:T(4,128)S(1)}, f32[2560,512,4]{1,0,2:T(8,128)S(1)}) fusion(pred[512,2560]{0,1:T(8,128)(4,1)S(1)} %pad_add_fusion.2, bf16[1536,4,64]{0,2,1:T(8,128)(2,1)} %get-tuple-element.192, s32[]{:T(128)S(6)} %select_n.119, bf16[1,512,64]{1,2,0:T(8,128)(2,1)S(1)} %copy-done.10, bf16[1,2048,64]{1,2,0:T(8,128)(2,1)S(1)} %copy-done.5), kind=kOutput, calls=%fused_computation.2.clone.1 | convolution fusion | flops 687470592 | bytes 22880260 | tf_op jit(solution)/shard_map/while/body/eval_jaxpr/rgke,gse->gkrs/dot_general | solution.py:61
  216.1 5.2 %fusion.94 = f32[4,512]{1,0:T(4,128)S(1)} fusion(f32[2560,512,4]{1,0,2:T(8,128)S(1)} %get-tuple-element.155, f32[4,512]{1,0:T(4,128)S(1)} %get-tuple-element.156, pred[512,2560]{0,1:T(8,128)(4,1)S(1)} %pad_add_fusion.2), kind=kLoop, calls=%fused_computation.3.clone.1 | loop fusion | flops 26212352 | bytes 22298624 | tf_op jit(solution)/shard_map/while/body/eval_jaxpr/reduce_sum | solution.py:75
  221.3 5.9 %fusion.96 = bf16[512,1,4,64]{0,3,2,1:T(8,128)(2,1)S(1)} fusion(f32[2560,512,4]{1,0,2:T(8,128)S(1)} %get-tuple-element.155, f32[4,512]{1,0:T(4,128)S(1)} %get-tuple-element.156, pred[512,2560]{0,1:T(8,128)(4,1)S(1)} %pad_add_fusion.2, bf16[1,512,64]{1,2,0:T(8,128)(2,1)S(1)} %get-tuple-element.157, bf16[1,2048,64]{1,2,0:T(8,128)(2,1)S(1)} %copy.39, ...), kind=kOutput, calls=%fused_computation.17.clone.1 | convolution fusion | flops 698220544 | bytes 22888448 | tf_op jit(solution)/shard_map/while/body/eval_jaxpr/gkrs,gse->rgke/dot_general | solution.py:78
  236.2 49.3 %reduce-scatter.3.cloned.1.call-done = bf16[128,2048]{1,0:T(8,128)(2,1)} async-done(((bf16[1024,2048]{1,0:T(8,128)(2,1)}), bf16[128,2048]{1,0:T(8,128)(2,1)}) %reduce-scatter.3.cloned.1.call-update) | async-done | bytes 524304 | tf_op jit(solution)/shard_map/reduce_scatter | solution.py:163
  288.9 46.0 %all-gather.8.cloned.1.call-done = bf16[512,2048]{1,0:T(8,128)(2,1)} async-done(((bf16[128,2048]{1,0:T(8,128)(2,1)}), bf16[512,2048]{1,0:T(8,128)(2,1)}) %all-gather.8.cloned.1.call-update) | async-done | bytes 2097168 | tf_op jit(solution)/shard_map/all_gather | solution.py:171
  334.9 6.5 %fusion.73 = f32[512,1024]{1,0:T(8,128)} fusion(bf16[512,2048]{1,0:T(8,128)(2,1)} %all-gather.8.cloned.1.call-done, bf16[2048,1024]{1,0:T(8,128)(2,1)} %param.27), kind=kOutput, calls=%fused_computation.120 | convolution fusion | flops 2147483648 | bytes 8388608 | tf_op jit(solution)/shard_map/dot_general | solution.py:172
  341.4 10.6 %convolution_convert_fusion.1 = bf16[512,2048]{1,0:T(8,128)(2,1)} fusion(bf16[1024,2048]{1,0:T(8,128)(2,1)} %param.29, f32[512,1024]{1,0:T(8,128)} %fusion.73, bf16[512,2048]{1,0:T(8,128)(2,1)} %all-gather.8.cloned.1.call-done, bf16[2048,1024]{1,0:T(8,128)(2,1)} %param.28), kind=kOutput, calls=%fused_computation.40 | convolution fusion | flops 4299161600 | bytes 14680064 | tf_op jit(solution)/shard_map/dot_general | solution.py:176
  352.1 42.7 %reduce-scatter.5.cloned.1.call-done = bf16[128,2048]{1,0:T(8,128)(2,1)} async-done(((bf16[512,2048]{1,0:T(8,128)(2,1)}), bf16[128,2048]{1,0:T(8,128)(2,1)}) %reduce-scatter.5.cloned.1.call-update) | async-done | bytes 524304 | tf_op jit(solution)/shard_map/reduce_scatter | solution.py:175
  396.3 23.8 %psum.14 = bf16[4,2048]{1,0:T(4,128)(2,1)S(1)} all-reduce(bf16[4,2048]{1,0:T(4,128)(2,1)S(1)} %convolution_convert_fusion.2), channel_id=1, replica_groups=mesh['req'=4,'tok'=8] {'tok'}, use_global_device_ids=true, to_apply=%region_11.12 | all-reduce | flops 8192 | bytes 32768 | tf_op jit(solution)/shard_map/psum | solution.py:185
  420.8 10.3 %fusion.72 = (f32[4]{0:T(128)S(1)}, f32[4,4000]{1,0:T(4,128)S(1)}) fusion(bf16[4000,2048]{1,0:T(8,128)(2,1)} %param.31, bf16[4,2048]{1,0:T(4,128)(2,1)S(1)} %psum.14, f32[2048]{0:T(1024)S(1)} %convert_element_type.108, f32[4]{0:T(128)S(1)} %get-tuple-element.92), kind=kOutput, calls=%fused_computation.119 | convolution fusion | flops 65584764 | bytes 16472608 | tf_op jit(solution)/shard_map/dot_general | solution.py:191
  431.1 11.8 %pmax.7 = f32[4]{0:T(128)S(1)} all-reduce(f32[4]{0:T(128)S(1)} %get-tuple-element.96), channel_id=1, replica_groups=mesh['req'=4,'tok'=8] {'tok'}, use_global_device_ids=true, to_apply=%region_14.15 | all-reduce | flops 4 | bytes 32 | tf_op jit(solution)/shard_map/pmax | solution.py:194
  443.8 11.8 %psum.15 = f32[4]{0:T(128)S(1)} all-reduce(f32[4]{0:T(128)S(1)} %exponential_reduce_fusion), channel_id=1, replica_groups=mesh['req'=4,'tok'=8] {'tok'}, use_global_device_ids=true, to_apply=%region_16.17 | all-reduce | flops 4 | bytes 32 | tf_op jit(solution)/shard_map/psum | solution.py:195
  (186 shorter events, 94.9 us)
Async XLA Ops:
  7.2 44.7 %copy-start = (bf16[4,2048,128]{2,1,0:T(8,128)(2,1)S(1)}, bf16[4,2048,128]{2,1,0:T(8,128)(2,1)}, u32[]{:S(2)}) copy-start(bf16[4,2048,128]{2,1,0:T(8,128)(2,1)} %param.24) | copy-start | bytes 6291460
  7.2 33.1 %all-gather.4.cloned.1.call-start = ((), (), s32[]{:S(2)}) async-start(), calls=%async_computation.3 | async-start | bytes 1310720 | tf_op jit(solution)/shard_map/all_gather | solution.py:131
  7.9 84.9 %all-gather.6.cloned.1.call-start = ((), (), s32[]{:S(2)}) async-start(), calls=%async_computation.4 | async-start | bytes 4718592 | tf_op jit(solution)/shard_map/all_gather | solution.py:118
  41.7 6.9 %copy-start.17 = (s32[4]{0:T(128)S(1)}, s32[4]{0:T(128)}, u32[]{:S(2)}) copy-start(s32[4]{0:T(128)} %param.20) | copy-start | bytes 52
  41.8 6.9 %copy-start.18 = (s32[1,4]{1,0:T(1,128)S(1)}, s32[1,4]{1,0:T(1,128)}, u32[]{:S(2)}) copy-start(s32[1,4]{1,0:T(1,128)} %param.19) | copy-start | bytes 52
  43.4 37.7 %all-to-all-start = ((bf16[4,8,256,128]{2,3,0,1:T(8,128)(2,1)}), bf16[4,8,256,128]{2,3,0,1:T(8,128)(2,1)}, u32[]{:S(2)}, u32[]{:S(2)}) async-start(bf16[4,8,256,128]{2,3,0,1:T(8,128)(2,1)} %bitcast.128), calls=%async_computation | async-start | bytes 4194304 | tf_op jit(solution)/shard_map/all_to_all | solution.py:133
  47.8 237.7 %reduce-scatter.3.cloned.1.call-start = ((), (), s32[]{:S(2)}) async-start(), calls=%async_computation.5 | async-start | bytes 4718592 | tf_op jit(solution)/shard_map/reduce_scatter | solution.py:163
  103.4 8.0 %copy-start.11 = (pred[512]{0:T(512)(128)(4,1)}, pred[512]{0:T(512)(128)(4,1)S(1)}, u32[]{:S(2)}) copy-start(pred[512]{0:T(512)(128)(4,1)S(1)} %iota_compare_fusion.9) | copy-start | bytes 1540 | tf_op jit(solution)/shard_map/while
  123.5 5.9 %copy-start.3 = (bf16[1536,256]{0,1:T(8,128)(2,1)S(1)}, bf16[1536,256]{0,1:T(8,128)(2,1)}, u32[]{:S(2)}) copy-start(bf16[1536,256]{0,1:T(8,128)(2,1)} %get-tuple-element.173) | copy-start | bytes 2359300 | tf_op jit(solution)/shard_map/while
  135.5 8.0 %copy-start.11 = (pred[512]{0:T(512)(128)(4,1)}, pred[512]{0:T(512)(128)(4,1)S(1)}, u32[]{:S(2)}) copy-start(pred[512]{0:T(512)(128)(4,1)S(1)} %iota_compare_fusion.9) | copy-start | bytes 1540 | tf_op jit(solution)/shard_map/while
  168.3 8.0 %copy-start.11 = (pred[512]{0:T(512)(128)(4,1)}, pred[512]{0:T(512)(128)(4,1)S(1)}, u32[]{:S(2)}) copy-start(pred[512]{0:T(512)(128)(4,1)S(1)} %iota_compare_fusion.9) | copy-start | bytes 1540 | tf_op jit(solution)/shard_map/while
  188.5 5.9 %copy-start.3 = (bf16[1536,256]{0,1:T(8,128)(2,1)S(1)}, bf16[1536,256]{0,1:T(8,128)(2,1)}, u32[]{:S(2)}) copy-start(bf16[1536,256]{0,1:T(8,128)(2,1)} %get-tuple-element.173) | copy-start | bytes 2359300 | tf_op jit(solution)/shard_map/while
  201.1 8.0 %copy-start.11 = (pred[512]{0:T(512)(128)(4,1)}, pred[512]{0:T(512)(128)(4,1)S(1)}, u32[]{:S(2)}) copy-start(pred[512]{0:T(512)(128)(4,1)S(1)} %iota_compare_fusion.9) | copy-start | bytes 1540 | tf_op jit(solution)/shard_map/while
  221.3 5.9 %copy-start.3 = (bf16[1536,256]{0,1:T(8,128)(2,1)S(1)}, bf16[1536,256]{0,1:T(8,128)(2,1)}, u32[]{:S(2)}) copy-start(bf16[1536,256]{0,1:T(8,128)(2,1)} %get-tuple-element.173) | copy-start | bytes 2359300 | tf_op jit(solution)/shard_map/while
  231.4 54.0 %copy-start.2 = (bf16[128,2048]{1,0:T(8,128)(2,1)S(1)}, bf16[128,2048]{1,0:T(8,128)(2,1)}, u32[]{:S(2)}) copy-start(bf16[128,2048]{1,0:T(8,128)(2,1)} %param.17) | copy-start | bytes 1572868
  236.1 98.8 %all-gather.8.cloned.1.call-start = ((), (), s32[]{:S(2)}) async-start(), calls=%async_computation.6 | async-start | bytes 2621440 | tf_op jit(solution)/shard_map/all_gather | solution.py:171
  288.8 106.0 %reduce-scatter.5.cloned.1.call-start = ((), (), s32[]{:S(2)}) async-start(), calls=%async_computation.7 | async-start | bytes 2621440 | tf_op jit(solution)/shard_map/reduce_scatter | solution.py:175
  341.4 10.7 %copy-start.14 = (bf16[2048]{0:T(1024)(128)(2,1)S(1)}, bf16[2048]{0:T(1024)(128)(2,1)}, u32[]{:S(2)}) copy-start(bf16[2048]{0:T(1024)(128)(2,1)} %param.30) | copy-start | bytes 12292
  341.4 53.4 %copy-start.6 = (bf16[128,2048]{1,0:T(8,128)(2,1)S(1)}, bf16[128,2048]{1,0:T(8,128)(2,1)}, u32[]{:S(2)}) copy-start(bf16[128,2048]{1,0:T(8,128)(2,1)} %reduce-scatter.3.cloned.1.call-done) | copy-start | bytes 1572868
  352.0 44.1 %copy-start.15 = (s32[4]{0:T(128)S(1)}, s32[4]{0:T(128)}, u32[]{:S(2)}) copy-start(s32[4]{0:T(128)} %get-tuple-element.94) | copy-start | bytes 52
  396.1 35.0 %copy-start.7 = (bf16[128,2048]{1,0:T(8,128)(2,1)}, bf16[128,2048]{1,0:T(8,128)(2,1)S(1)}, u32[]{:S(2)}) copy-start(bf16[128,2048]{1,0:T(8,128)(2,1)S(1)} %fusion.45) | copy-start | bytes 1572868
  420.8 22.3 %copy-start.9 = (bf16[1024,1,128]{0,2,1:T(8,128)(2,1)S(1)}, bf16[1024,1,128]{0,2,1:T(8,128)(2,1)}, u32[]{:S(2)}) copy-start(bf16[1024,1,128]{0,2,1:T(8,128)(2,1)} %copy-done.8) | copy-start | bytes 786436
  420.8 35.3 %copy-start.1 = (bf16[4,2048,128]{2,1,0:T(8,128)(2,1)S(1)}, bf16[4,2048,128]{2,1,0:T(8,128)(2,1)}, u32[]{:S(2)}) copy-start(bf16[4,2048,128]{2,1,0:T(8,128)(2,1)} %param.24) | copy-start | bytes 6291460
  442.9 13.2 %copy-start.16 = (f32[4]{0:T(128)}, f32[4]{0:T(128)S(1)}, u32[]{:S(2)}) copy-start(f32[4]{0:T(128)S(1)} %pmax.7) | copy-start | bytes 52
  (19 other events, 43.5 us)
Sparse Core Ops, SparseCore 0:
  9.6 30.6 all-gather.3
  42.7 50.0 all-gather.5
  236.2 49.1 reduce-scatter.2
  289.0 45.9 all-gather.7
  352.2 42.5 reduce-scatter.4
where the time goes:
time: 464 us; the launch traced here: 463 us
  waiting for transfers between devices  205 us (44%)
  matrix products  79 us (17%)
  local copies, waits for them, and re-layouts  50.9 us (11%)
  blocking collectives  47.4 us (10%)
  other arithmetic  45.6 us (10%)
  loops' own time  16.2 us (3%)
  between operations  14 us (3%)
    reduce_scatter x1, waiting for transfers between devices, shards(): lax.psum_scatter(jnp.dot(attended, out_weight, preferred_element_type=jnp...  49.3 us
    all_gather x1, waiting for transfers between devices, shards(): shard_part = lax.all_gather(mlp_in, 'req', axis=0, tiled=True)  46 us
    reduce_scatter x1, waiting for transfers between devices, shards(): lax.psum_scatter(jnp.dot(hidden_act, down_weight, preferred_element_type=...  42.7 us
    all_to_all x1, waiting for transfers between devices, shards(): lax.all_to_all(routed, 'tok', split_axis=1, concat_axis=2, tiled=True)  29.2 us
    all_gather x1, waiting for transfers between devices, shards(): every_owner = lax.all_gather(prefix_cache, 'req', axis=0, tiled=True)  28.3 us
    psum x1, blocking collectives, shards(): last_rows = lax.psum(picked.astype(jnp.bfloat16), 'tok').astype(jnp.float32)  23.8 us
    dot_general x4, matrix products, request_attention(): jnp.einsum('gkrs,gse->rgke', rounded, value_rows, preferred_element_type=...  23.7 us
    reduce_sum x4, other arithmetic, request_attention(): totals = jnp.sum(weights, axis=-1, keepdims=True)  20.8 us
  transfers between devices with their start and end apart: 6, of which 6 were waited for; matrix products, arithmetic and copies ran while one was open for 3% of the time, Pallas kernels for 0%

commit v1 on v0

--- a/solution.py
+++ b/solution.py
@@ -8,6 +8,22 @@
 PRE_LEN = 16384
 epsilon = 1e-05
 neg_large = -1e30
+
+
+def ring_gather(x, axis, dim):
+    ways, here, step = (lax.axis_size(axis), lax.axis_index(axis), x.shape[dim])
+    dims = [n * ways if d == dim else n for d, n in enumerate(x.shape)]
+    full = lax.dynamic_update_slice_in_dim(jnp.zeros(dims, x.dtype), x, here * step, axis=dim)
+    going_up = going_down = x
+    for far in range(1, ways // 2 + 1):
+        going_up = lax.ppermute(going_up, axis, [(d, (d + 1) % ways) for d in range(ways)])
+        full = lax.dynamic_update_slice_in_dim(full, going_up, (here - far) % ways * step, axis=dim)
+        if 2 * far < ways:
+            going_down = lax.ppermute(going_down, axis, [(d, (d - 1) % ways) for d in range(ways)])
+            full = lax.dynamic_update_slice_in_dim(
+                full, going_down, (here + far) % ways * step, axis=dim
+            )
+    return full
 
 
 def rms_scale(values, gain_vec):
@@ -128,7 +144,7 @@
     cache_width = kv_count * 2 * HD // tok_count
     cache_offset = tok_place * cache_width % (2 * HD)
     suffix_cache = lax.dynamic_slice_in_dim(keyvals[:, 0, :], cache_offset, cache_width, 1)
-    every_owner = lax.all_gather(prefix_cache, "req", axis=0, tiled=True)
+    every_owner = ring_gather(prefix_cache, "req", 0)
     routed = jnp.repeat(every_owner, repeat_count, axis=1)
     windows = lax.all_to_all(routed, "tok", split_axis=1, concat_axis=2, tiled=True)
     windows = windows[:, 0]

time: 464 us -> 448 us (0.966)
  waiting for transfers between devices: 205 us -> 179 us
  starting transfers between devices: 4.54 us -> 9.68 us
  local copies, waits for them, and re-layouts: 50.9 us -> 55.7 us
    all_gather x1 -> x0, waiting for transfers between devices: 28.3 us -> none  [shards(): every_owner = lax.all_gather(prefix_cache, 'req', axis=0, tiled=True)]
    ppermute x0 -> x3, waiting for transfers between devices: none -> 12.6 us  [the longest x2 9.5 us: ring_gather(): lax.ppermute(going_up, axis, [(d, (d + 1) % ways) for d in range(ways)])]
    all_gather x1, waiting for transfers between devices: 8.7 us -> 0.02 us  [shards(): lax.all_gather(normed, 'tok', axis=0, tiled=True)]
    ppermute x0 -> x3, starting transfers between devices: none -> 5.17 us  [the longest x2 3.08 us: ring_gather(): lax.ppermute(going_up, axis, [(d, (d + 1) % ways) for d in range(ways)])]
  transfers between devices with their start and end apart: 6 -> 8, of which waited for: 6 -> 7; matrix products, arithmetic and copies ran while one was open for 3% -> 3% of each run, Pallas kernels for 0% -> 0%
where the time goes in v1:
time: 448 us; the launch traced here: 446 us
  waiting for transfers between devices  179 us (40%)
  matrix products  79 us (18%)
  local copies, waits for them, and re-layouts  55.7 us (12%)
  blocking collectives  47.4 us (11%)
  other arithmetic  45.7 us (10%)
  loops' own time  16.2 us (4%)
  between operations  14.1 us (3%)
  starting transfers between devices  9.68 us (2%)
    reduce_scatter x1, waiting for transfers between devices, shards(): lax.psum_scatter(jnp.dot(attended, out_weight, preferred_element_type=jnp...  50.1 us
    all_gather x1, waiting for transfers between devices, shards(): shard_part = lax.all_gather(mlp_in, 'req', axis=0, tiled=True)  46 us
    reduce_scatter x1, waiting for transfers between devices, shards(): lax.psum_scatter(jnp.dot(hidden_act, down_weight, preferred_element_type=...  42.7 us
    all_to_all x1, waiting for transfers between devices, shards(): lax.all_to_all(routed, 'tok', split_axis=1, concat_axis=2, tiled=True)  27.1 us
    psum x1, blocking collectives, shards(): last_rows = lax.psum(picked.astype(jnp.bfloat16), 'tok').astype(jnp.float32)  23.8 us
    dot_general x4, matrix products, request_attention(): jnp.einsum('gkrs,gse->rgke', rounded, value_rows, preferred_element_type=...  23.7 us
    reduce_sum x4, other arithmetic, request_attention(): totals = jnp.sum(weights, axis=-1, keepdims=True)  20.8 us
    dot_general x4, matrix products, request_attention(): jnp.einsum('rgke,gse->gkrs', query_block, key_rows, preferred_element_typ...  18.7 us
  transfers between devices with their start and end apart: 8, of which 7 were waited for; matrix products, arithmetic and copies ran while one was open for 3% of the time, Pallas kernels for 0%

profile of v1, /device:TPU:0, one launch (start us, length us, event | category | flops | bytes accessed | tf_op | source)
XLA Modules:
  0.0 446.4 jit_solution(2747676593115399365)
XLA Ops:
  17.6 6.3 %collective-permute-done = bf16[1,4,256,128]{3,2,1,0:T(8,128)(2,1)} collective-permute-done((bf16[1,4,256,128]{3,2,1,0:T(8,128)(2,1)}, bf16[1,4,256,128]{3,2,1,0:T(8,128)(2,1)}, u32[]{:S(2)}, u32[]{:S(2)}) %collective-permute-start) | collective-permute-done | bytes 262176 | tf_op jit(solution)/shard_map/ppermute | solution.py:19
  45.6 27.1 %all-to-all-done = bf16[4,8,256,128]{2,3,0,1:T(8,128)(2,1)} async-done(((bf16[4,8,256,128]{2,3,0,1:T(8,128)(2,1)}), bf16[4,8,256,128]{2,3,0,1:T(8,128)(2,1)}, u32[]{:S(2)}, u32[]{:S(2)}) %all-to-all-start) | async-done | bytes 2097184 | tf_op jit(solution)/shard_map/all_to_all | solution.py:149
  84.4 129.9 %while.10 = (s32[]{:T(128)}, bf16[1536,256]{0,1:T(8,128)(2,1)}, s32[4]{0:T(128)}, s32[4]{0:T(128)}, bf16[4,2048,128]{2,1,0:T(8,128)(2,1)S(1)}, /*index=5*/s32[4]...) while((s32[]{:T(128)}, bf16[1536,256]{0,1:T(8,128)(2,1)}, ...), condition=%wide.region_7.8_spmd, body=%wide.region_4.7_spmd.sunk | while | flops 1415707136 | bytes 83556792 | solution.py:177
  96.6 4.7 %fusion.93 = (f32[4,512]{1,0:T(4,128)S(1)}, f32[2560,512,4]{1,0,2:T(8,128)S(1)}) fusion(pred[512,2560]{0,1:T(8,128)(4,1)S(1)} %pad_add_fusion.2, bf16[1536,4,64]{0,2,1:T(8,128)(2,1)} %get-tuple-element.192, s32[]{:T(128)S(6)} %select_n.150, bf16[1,512,64]{1,2,0:T(8,128)(2,1)S(1)} %copy-done.10, bf16[1,2048,64]{1,2,0:T(8,128)(2,1)S(1)} %copy-done.5), kind=kOutput, calls=%fused_computation.2.clone.1 | convolution fusion | flops 687470592 | bytes 22880260 | tf_op jit(solution)/shard_map/while/body/eval_jaxpr/rgke,gse->gkrs/dot_general | solution.py:77
  101.3 5.2 %fusion.94 = f32[4,512]{1,0:T(4,128)S(1)} fusion(f32[2560,512,4]{1,0,2:T(8,128)S(1)} %get-tuple-element.155, f32[4,512]{1,0:T(4,128)S(1)} %get-tuple-element.156, pred[512,2560]{0,1:T(8,128)(4,1)S(1)} %pad_add_fusion.2), kind=kLoop, calls=%fused_computation.3.clone.1 | loop fusion | flops 26212352 | bytes 22298624 | tf_op jit(solution)/shard_map/while/body/eval_jaxpr/reduce_sum | solution.py:91
  106.5 5.9 %fusion.96 = bf16[512,1,4,64]{0,3,2,1:T(8,128)(2,1)S(1)} fusion(f32[2560,512,4]{1,0,2:T(8,128)S(1)} %get-tuple-element.155, f32[4,512]{1,0:T(4,128)S(1)} %get-tuple-element.156, pred[512,2560]{0,1:T(8,128)(4,1)S(1)} %pad_add_fusion.2, bf16[1,512,64]{1,2,0:T(8,128)(2,1)S(1)} %get-tuple-element.157, bf16[1,2048,64]{1,2,0:T(8,128)(2,1)S(1)} %copy.51, ...), kind=kOutput, calls=%fused_computation.17.clone.1 | convolution fusion | flops 698220544 | bytes 22888448 | tf_op jit(solution)/shard_map/while/body/eval_jaxpr/gkrs,gse->rgke/dot_general | solution.py:94
  128.7 4.7 %fusion.93 = (f32[4,512]{1,0:T(4,128)S(1)}, f32[2560,512,4]{1,0,2:T(8,128)S(1)}) fusion(pred[512,2560]{0,1:T(8,128)(4,1)S(1)} %pad_add_fusion.2, bf16[1536,4,64]{0,2,1:T(8,128)(2,1)} %get-tuple-element.192, s32[]{:T(128)S(6)} %select_n.150, bf16[1,512,64]{1,2,0:T(8,128)(2,1)S(1)} %copy-done.10, bf16[1,2048,64]{1,2,0:T(8,128)(2,1)S(1)} %copy-done.5), kind=kOutput, calls=%fused_computation.2.clone.1 | convolution fusion | flops 687470592 | bytes 22880260 | tf_op jit(solution)/shard_map/while/body/eval_jaxpr/rgke,gse->gkrs/dot_general | solution.py:77
  133.4 5.2 %fusion.94 = f32[4,512]{1,0:T(4,128)S(1)} fusion(f32[2560,512,4]{1,0,2:T(8,128)S(1)} %get-tuple-element.155, f32[4,512]{1,0:T(4,128)S(1)} %get-tuple-element.156, pred[512,2560]{0,1:T(8,128)(4,1)S(1)} %pad_add_fusion.2), kind=kLoop, calls=%fused_computation.3.clone.1 | loop fusion | flops 26212352 | bytes 22298624 | tf_op jit(solution)/shard_map/while/body/eval_jaxpr/reduce_sum | solution.py:91
  138.7 5.9 %fusion.96 = bf16[512,1,4,64]{0,3,2,1:T(8,128)(2,1)S(1)} fusion(f32[2560,512,4]{1,0,2:T(8,128)S(1)} %get-tuple-element.155, f32[4,512]{1,0:T(4,128)S(1)} %get-tuple-element.156, pred[512,2560]{0,1:T(8,128)(4,1)S(1)} %pad_add_fusion.2, bf16[1,512,64]{1,2,0:T(8,128)(2,1)S(1)} %get-tuple-element.157, bf16[1,2048,64]{1,2,0:T(8,128)(2,1)S(1)} %copy.51, ...), kind=kOutput, calls=%fused_computation.17.clone.1 | convolution fusion | flops 698220544 | bytes 22888448 | tf_op jit(solution)/shard_map/while/body/eval_jaxpr/gkrs,gse->rgke/dot_general | solution.py:94
  161.5 4.7 %fusion.93 = (f32[4,512]{1,0:T(4,128)S(1)}, f32[2560,512,4]{1,0,2:T(8,128)S(1)}) fusion(pred[512,2560]{0,1:T(8,128)(4,1)S(1)} %pad_add_fusion.2, bf16[1536,4,64]{0,2,1:T(8,128)(2,1)} %get-tuple-element.192, s32[]{:T(128)S(6)} %select_n.150, bf16[1,512,64]{1,2,0:T(8,128)(2,1)S(1)} %copy-done.10, bf16[1,2048,64]{1,2,0:T(8,128)(2,1)S(1)} %copy-done.5), kind=kOutput, calls=%fused_computation.2.clone.1 | convolution fusion | flops 687470592 | bytes 22880260 | tf_op jit(solution)/shard_map/while/body/eval_jaxpr/rgke,gse->gkrs/dot_general | solution.py:77
  166.2 5.2 %fusion.94 = f32[4,512]{1,0:T(4,128)S(1)} fusion(f32[2560,512,4]{1,0,2:T(8,128)S(1)} %get-tuple-element.155, f32[4,512]{1,0:T(4,128)S(1)} %get-tuple-element.156, pred[512,2560]{0,1:T(8,128)(4,1)S(1)} %pad_add_fusion.2), kind=kLoop, calls=%fused_computation.3.clone.1 | loop fusion | flops 26212352 | bytes 22298624 | tf_op jit(solution)/shard_map/while/body/eval_jaxpr/reduce_sum | solution.py:91
  171.5 5.9 %fusion.96 = bf16[512,1,4,64]{0,3,2,1:T(8,128)(2,1)S(1)} fusion(f32[2560,512,4]{1,0,2:T(8,128)S(1)} %get-tuple-element.155, f32[4,512]{1,0:T(4,128)S(1)} %get-tuple-element.156, pred[512,2560]{0,1:T(8,128)(4,1)S(1)} %pad_add_fusion.2, bf16[1,512,64]{1,2,0:T(8,128)(2,1)S(1)} %get-tuple-element.157, bf16[1,2048,64]{1,2,0:T(8,128)(2,1)S(1)} %copy.51, ...), kind=kOutput, calls=%fused_computation.17.clone.1 | convolution fusion | flops 698220544 | bytes 22888448 | tf_op jit(solution)/shard_map/while/body/eval_jaxpr/gkrs,gse->rgke/dot_general | solution.py:94
  194.3 4.7 %fusion.93 = (f32[4,512]{1,0:T(4,128)S(1)}, f32[2560,512,4]{1,0,2:T(8,128)S(1)}) fusion(pred[512,2560]{0,1:T(8,128)(4,1)S(1)} %pad_add_fusion.2, bf16[1536,4,64]{0,2,1:T(8,128)(2,1)} %get-tuple-element.192, s32[]{:T(128)S(6)} %select_n.150, bf16[1,512,64]{1,2,0:T(8,128)(2,1)S(1)} %copy-done.10, bf16[1,2048,64]{1,2,0:T(8,128)(2,1)S(1)} %copy-done.5), kind=kOutput, calls=%fused_computation.2.clone.1 | convolution fusion | flops 687470592 | bytes 22880260 | tf_op jit(solution)/shard_map/while/body/eval_jaxpr/rgke,gse->gkrs/dot_general | solution.py:77
  199.0 5.2 %fusion.94 = f32[4,512]{1,0:T(4,128)S(1)} fusion(f32[2560,512,4]{1,0,2:T(8,128)S(1)} %get-tuple-element.155, f32[4,512]{1,0:T(4,128)S(1)} %get-tuple-element.156, pred[512,2560]{0,1:T(8,128)(4,1)S(1)} %pad_add_fusion.2), kind=kLoop, calls=%fused_computation.3.clone.1 | loop fusion | flops 26212352 | bytes 22298624 | tf_op jit(solution)/shard_map/while/body/eval_jaxpr/reduce_sum | solution.py:91
  204.3 5.9 %fusion.96 = bf16[512,1,4,64]{0,3,2,1:T(8,128)(2,1)S(1)} fusion(f32[2560,512,4]{1,0,2:T(8,128)S(1)} %get-tuple-element.155, f32[4,512]{1,0:T(4,128)S(1)} %get-tuple-element.156, pred[512,2560]{0,1:T(8,128)(4,1)S(1)} %pad_add_fusion.2, bf16[1,512,64]{1,2,0:T(8,128)(2,1)S(1)} %get-tuple-element.157, bf16[1,2048,64]{1,2,0:T(8,128)(2,1)S(1)} %copy.51, ...), kind=kOutput, calls=%fused_computation.17.clone.1 | convolution fusion | flops 698220544 | bytes 22888448 | tf_op jit(solution)/shard_map/while/body/eval_jaxpr/gkrs,gse->rgke/dot_general | solution.py:94
  219.1 50.1 %reduce-scatter.3.cloned.1.call-done = bf16[128,2048]{1,0:T(8,128)(2,1)} async-done(((bf16[1024,2048]{1,0:T(8,128)(2,1)}), bf16[128,2048]{1,0:T(8,128)(2,1)}) %reduce-scatter.3.cloned.1.call-update) | async-done | bytes 524304 | tf_op jit(solution)/shard_map/reduce_scatter | solution.py:179
  272.6 46.0 %all-gather.5.cloned.1.call-done = bf16[512,2048]{1,0:T(8,128)(2,1)} async-done(((bf16[128,2048]{1,0:T(8,128)(2,1)}), bf16[512,2048]{1,0:T(8,128)(2,1)}) %all-gather.5.cloned.1.call-update) | async-done | bytes 2097168 | tf_op jit(solution)/shard_map/all_gather | solution.py:187
  318.7 6.5 %fusion.73 = f32[512,1024]{1,0:T(8,128)} fusion(bf16[512,2048]{1,0:T(8,128)(2,1)} %all-gather.5.cloned.1.call-done, bf16[2048,1024]{1,0:T(8,128)(2,1)} %param.27), kind=kOutput, calls=%fused_computation.124 | convolution fusion | flops 2147483648 | bytes 8388608 | tf_op jit(solution)/shard_map/dot_general | solution.py:188
  325.1 10.6 %convolution_convert_fusion.1 = bf16[512,2048]{1,0:T(8,128)(2,1)} fusion(bf16[1024,2048]{1,0:T(8,128)(2,1)} %param.29, f32[512,1024]{1,0:T(8,128)} %fusion.73, bf16[512,2048]{1,0:T(8,128)(2,1)} %all-gather.5.cloned.1.call-done, bf16[2048,1024]{1,0:T(8,128)(2,1)} %param.28), kind=kOutput, calls=%fused_computation.40 | convolution fusion | flops 4299161600 | bytes 14680064 | tf_op jit(solution)/shard_map/dot_general | solution.py:192
  335.9 42.7 %reduce-scatter.5.cloned.1.call-done = bf16[128,2048]{1,0:T(8,128)(2,1)} async-done(((bf16[512,2048]{1,0:T(8,128)(2,1)}), bf16[128,2048]{1,0:T(8,128)(2,1)}) %reduce-scatter.5.cloned.1.call-update) | async-done | bytes 524304 | tf_op jit(solution)/shard_map/reduce_scatter | solution.py:191
  380.1 23.8 %psum.14 = bf16[4,2048]{1,0:T(4,128)(2,1)S(1)} all-reduce(bf16[4,2048]{1,0:T(4,128)(2,1)S(1)} %convolution_convert_fusion.2), channel_id=1, replica_groups=mesh['req'=4,'tok'=8] {'tok'}, use_global_device_ids=true, to_apply=%region_11.12 | all-reduce | flops 8192 | bytes 32768 | tf_op jit(solution)/shard_map/psum | solution.py:201
  404.6 10.3 %fusion.72 = (f32[4]{0:T(128)S(1)}, f32[4,4000]{1,0:T(4,128)S(1)}) fusion(bf16[4000,2048]{1,0:T(8,128)(2,1)} %param.31, bf16[4,2048]{1,0:T(4,128)(2,1)S(1)} %psum.14, f32[2048]{0:T(1024)S(1)} %convert_element_type.108, f32[4]{0:T(128)S(1)} %get-tuple-element.92), kind=kOutput, calls=%fused_computation.123 | convolution fusion | flops 65584764 | bytes 16472608 | tf_op jit(solution)/shard_map/dot_general | solution.py:207
  414.9 11.8 %pmax.7 = f32[4]{0:T(128)S(1)} all-reduce(f32[4]{0:T(128)S(1)} %get-tuple-element.96), channel_id=1, replica_groups=mesh['req'=4,'tok'=8] {'tok'}, use_global_device_ids=true, to_apply=%region_14.15 | all-reduce | flops 4 | bytes 32 | tf_op jit(solution)/shard_map/pmax | solution.py:210
  427.6 11.8 %psum.15 = f32[4]{0:T(128)S(1)} all-reduce(f32[4]{0:T(128)S(1)} %exponential_reduce_fusion), channel_id=1, replica_groups=mesh['req'=4,'tok'=8] {'tok'}, use_global_device_ids=true, to_apply=%region_16.17 | all-reduce | flops 4 | bytes 32 | tf_op jit(solution)/shard_map/psum | solution.py:211
  (197 shorter events, 105.9 us)
Async XLA Ops:
  7.2 38.4 %copy-start = (bf16[4,2048,128]{2,1,0:T(8,128)(2,1)S(1)}, bf16[4,2048,128]{2,1,0:T(8,128)(2,1)}, u32[]{:S(2)}) copy-start(bf16[4,2048,128]{2,1,0:T(8,128)(2,1)} %param.24) | copy-start | bytes 6291460
  7.2 68.6 %all-gather.3.cloned.1.call-start = ((), (), s32[]{:S(2)}) async-start(), calls=%async_computation.3 | async-start | bytes 4718592 | tf_op jit(solution)/shard_map/all_gather | solution.py:134
  11.3 12.6 %collective-permute-start = (bf16[1,4,256,128]{3,2,1,0:T(8,128)(2,1)}, bf16[1,4,256,128]{3,2,1,0:T(8,128)(2,1)}, u32[]{:S(2)}, u32[]{:S(2)}) collective-permute-start(bf16[1,4,256,128]{3,2,1,0:T(8,128)(2,1)} %param.21), channel_id=1, source_target_pairs={{0,8},{8,16},{16,24},{24,0},{1,9},{9,17},{17,25},{25,1},{2,10},{10... | collective-permute-start | bytes 786440 | tf_op jit(solution)/shard_map/ppermute | solution.py:19
  14.4 13.9 %collective-permute-start.1 = (bf16[1,4,256,128]{3,2,1,0:T(8,128)(2,1)}, bf16[1,4,256,128]{3,2,1,0:T(8,128)(2,1)}, u32[]{:S(2)}, u32[]{:S(2)}) collective-permute-start(bf16[1,4,256,128]{3,2,1,0:T(8,128)(2,1)} %param.21), channel_id=1, source_target_pairs={{0,24},{8,0},{16,8},{24,16},{1,25},{9,1},{17,9},{25,17},{2,26},{10... | collective-permute-start | bytes 786440 | tf_op jit(solution)/shard_map/ppermute | solution.py:22
  23.9 10.4 %collective-permute-start.2 = (bf16[1,4,256,128]{3,2,1,0:T(8,128)(2,1)}, bf16[1,4,256,128]{3,2,1,0:T(8,128)(2,1)}, u32[]{:S(2)}, u32[]{:S(2)}) collective-permute-start(bf16[1,4,256,128]{3,2,1,0:T(8,128)(2,1)} %collective-permute-done), channel_id=1, source_target_pairs={{0,8},{8,16},{16,24},{24,0},{1,9},{9,17},{17,25},{25,1},{2,10},{10... | collective-permute-start | bytes 786440 | tf_op jit(solution)/shard_map/ppermute | solution.py:19
  31.1 11.2 %copy-start.17 = (s32[4]{0:T(128)S(1)}, s32[4]{0:T(128)}, u32[]{:S(2)}) copy-start(s32[4]{0:T(128)} %param.20) | copy-start | bytes 52
  31.1 11.2 %copy-start.18 = (s32[1,4]{1,0:T(1,128)S(1)}, s32[1,4]{1,0:T(1,128)}, u32[]{:S(2)}) copy-start(s32[1,4]{1,0:T(1,128)} %param.19) | copy-start | bytes 52
  37.1 35.6 %all-to-all-start = ((bf16[4,8,256,128]{2,3,0,1:T(8,128)(2,1)}), bf16[4,8,256,128]{2,3,0,1:T(8,128)(2,1)}, u32[]{:S(2)}, u32[]{:S(2)}) async-start(bf16[4,8,256,128]{2,3,0,1:T(8,128)(2,1)} %bitcast.128), calls=%async_computation | async-start | bytes 4194304 | tf_op jit(solution)/shard_map/all_to_all | solution.py:149
  41.5 227.7 %reduce-scatter.3.cloned.1.call-start = ((), (), s32[]{:S(2)}) async-start(), calls=%async_computation.4 | async-start | bytes 4718592 | tf_op jit(solution)/shard_map/reduce_scatter | solution.py:179
  86.3 8.0 %copy-start.11 = (pred[512]{0:T(512)(128)(4,1)}, pred[512]{0:T(512)(128)(4,1)S(1)}, u32[]{:S(2)}) copy-start(pred[512]{0:T(512)(128)(4,1)S(1)} %iota_compare_fusion.9) | copy-start | bytes 1540 | tf_op jit(solution)/shard_map/while
  118.5 8.0 %copy-start.11 = (pred[512]{0:T(512)(128)(4,1)}, pred[512]{0:T(512)(128)(4,1)S(1)}, u32[]{:S(2)}) copy-start(pred[512]{0:T(512)(128)(4,1)S(1)} %iota_compare_fusion.9) | copy-start | bytes 1540 | tf_op jit(solution)/shard_map/while
  151.3 8.0 %copy-start.11 = (pred[512]{0:T(512)(128)(4,1)}, pred[512]{0:T(512)(128)(4,1)S(1)}, u32[]{:S(2)}) copy-start(pred[512]{0:T(512)(128)(4,1)S(1)} %iota_compare_fusion.9) | copy-start | bytes 1540 | tf_op jit(solution)/shard_map/while
  171.5 5.9 %copy-start.3 = (bf16[1536,256]{0,1:T(8,128)(2,1)S(1)}, bf16[1536,256]{0,1:T(8,128)(2,1)}, u32[]{:S(2)}) copy-start(bf16[1536,256]{0,1:T(8,128)(2,1)} %get-tuple-element.173) | copy-start | bytes 2359300 | tf_op jit(solution)/shard_map/while
  184.1 8.0 %copy-start.11 = (pred[512]{0:T(512)(128)(4,1)}, pred[512]{0:T(512)(128)(4,1)S(1)}, u32[]{:S(2)}) copy-start(pred[512]{0:T(512)(128)(4,1)S(1)} %iota_compare_fusion.9) | copy-start | bytes 1540 | tf_op jit(solution)/shard_map/while
  214.4 54.9 %copy-start.2 = (bf16[128,2048]{1,0:T(8,128)(2,1)S(1)}, bf16[128,2048]{1,0:T(8,128)(2,1)}, u32[]{:S(2)}) copy-start(bf16[128,2048]{1,0:T(8,128)(2,1)} %param.17) | copy-start | bytes 1572868
  219.1 99.6 %all-gather.5.cloned.1.call-start = ((), (), s32[]{:S(2)}) async-start(), calls=%async_computation.5 | async-start | bytes 2621440 | tf_op jit(solution)/shard_map/all_gather | solution.py:187
  272.6 106.0 %reduce-scatter.5.cloned.1.call-start = ((), (), s32[]{:S(2)}) async-start(), calls=%async_computation.6 | async-start | bytes 2621440 | tf_op jit(solution)/shard_map/reduce_scatter | solution.py:191
  325.1 10.7 %copy-start.14 = (bf16[2048]{0:T(1024)(128)(2,1)S(1)}, bf16[2048]{0:T(1024)(128)(2,1)}, u32[]{:S(2)}) copy-start(bf16[2048]{0:T(1024)(128)(2,1)} %param.30) | copy-start | bytes 12292
  325.1 53.4 %copy-start.6 = (bf16[128,2048]{1,0:T(8,128)(2,1)S(1)}, bf16[128,2048]{1,0:T(8,128)(2,1)}, u32[]{:S(2)}) copy-start(bf16[128,2048]{1,0:T(8,128)(2,1)} %reduce-scatter.3.cloned.1.call-done) | copy-start | bytes 1572868
  335.8 44.1 %copy-start.15 = (s32[4]{0:T(128)S(1)}, s32[4]{0:T(128)}, u32[]{:S(2)}) copy-start(s32[4]{0:T(128)} %get-tuple-element.94) | copy-start | bytes 52
  379.8 35.0 %copy-start.7 = (bf16[128,2048]{1,0:T(8,128)(2,1)}, bf16[128,2048]{1,0:T(8,128)(2,1)S(1)}, u32[]{:S(2)}) copy-start(bf16[128,2048]{1,0:T(8,128)(2,1)S(1)} %fusion.45) | copy-start | bytes 1572868
  404.6 22.3 %copy-start.9 = (bf16[1024,1,128]{0,2,1:T(8,128)(2,1)S(1)}, bf16[1024,1,128]{0,2,1:T(8,128)(2,1)}, u32[]{:S(2)}) copy-start(bf16[1024,1,128]{0,2,1:T(8,128)(2,1)} %copy-done.8) | copy-start | bytes 786436
  404.6 35.3 %copy-start.1 = (bf16[4,2048,128]{2,1,0:T(8,128)(2,1)S(1)}, bf16[4,2048,128]{2,1,0:T(8,128)(2,1)}, u32[]{:S(2)}) copy-start(bf16[4,2048,128]{2,1,0:T(8,128)(2,1)} %param.24) | copy-start | bytes 6291460
  426.7 13.2 %copy-start.16 = (f32[4]{0:T(128)}, f32[4]{0:T(128)S(1)}, u32[]{:S(2)}) copy-start(f32[4]{0:T(128)S(1)} %pmax.7) | copy-start | bytes 52
  (21 other events, 55.4 us)
Sparse Core Ops, SparseCore 0:
  11.5 44.0 all-gather.2
  219.2 49.9 reduce-scatter.2
  272.7 45.9 all-gather.4
  335.9 42.5 reduce-scatter.4
